TPU v7x, 128 devices: a whole 4x4x4 slice. The times are simulated.
128 devices in a mesh: seq: 16 (over x, z), tp: 8 (over y, core).
Axes of the slice: x: 4, y: 4, z: 4, core: 2. Of those that a mesh axis runs over, the one named last changes fastest.
Arguments:
- queries: bfloat16 [4096, 8192], P('seq', 'tp'), may hold values from -1000 to 1000
- states: bfloat16 [8192, 4096], P('seq', 'tp'), may hold values from -18 to 18
- state_doc: int32 [8192], replicated, may hold values from 0 to 15, as said below
- state_pos: int32 [8192], replicated, may hold values from 0 to 511, as said below
- lengths: int32 [16], replicated, may hold values from 64 to 512, as said below
- offsets: int32 [16], replicated, may hold values from 0 to 256
- key_weight: bfloat16 [4096, 8192], P(None, 'tp'), may hold values from -1 to 1
- value_weight: bfloat16 [4096, 8192], P(None, 'tp'), may hold values from -1 to 1
- context_grad: bfloat16 [4096, 8192], P('seq', 'tp'), may hold values from -6 to 6
Outputs:
- query_grad: bfloat16 [4096, 8192], P('seq', 'tp')
- key_weight_grad: bfloat16 [4096, 8192], P('seq', 'tp')
- value_weight_grad: bfloat16 [4096, 8192], P('seq', 'tp')
Inputs may be any that keep to these rules, and one draw needn't show every extreme that they name: `state_doc`: each document has exactly 512 state rows. The 512 rows held by one index of seq name any one document at most 56 times, and in every draw some device's rows name some document exactly 56 times. `state_pos`: within one document the state rows carry each position from 0 to 511 exactly once. `lengths`: some document has length 512.
All inputs are finite; a program needn't handle non-finite values.
Results may differ from a plain program's by a relative error of at most 0.017.
Values may be sent and summed in bfloat16 or wider, within the bound.
A program may use at most 128 MiB of HBM per device.

v0:
```python
import jax
import jax.numpy as jnp
from jax import lax
from jax.sharding import PartitionSpec as P

HEAD_DIM = 128


def attend(query_rows, key_rows, value_rows, grad_rows, length, offset):
    query_count = query_rows.shape[0]
    state_count = key_rows.shape[0]
    head_count = query_rows.shape[1] // HEAD_DIM
    query_heads = query_rows.reshape(query_count, head_count, HEAD_DIM)
    key_heads = key_rows.reshape(state_count, head_count, HEAD_DIM)
    value_heads = value_rows.reshape(state_count, head_count, HEAD_DIM)
    grad_heads = grad_rows.reshape(query_count, head_count, HEAD_DIM)
    score_scale = HEAD_DIM ** (-0.5)
    scores = (
        jnp.einsum("qhd,khd->hqk", query_heads, key_heads, preferred_element_type=jnp.float32)
        * score_scale
    )
    query_index = jnp.arange(query_count)
    positions = jnp.arange(state_count)
    visible = (positions[None, :] <= offset + query_index[:, None]) & (positions[None, :] < length)
    scores = jnp.where(visible[None], scores, -jnp.inf)
    row_top = jnp.max(scores, axis=-1, keepdims=True)
    weights = jnp.exp(scores - row_top)
    probabilities = weights / jnp.sum(weights, axis=-1, keepdims=True)
    probs_low = probabilities.astype(jnp.bfloat16)
    context = jnp.einsum("hqk,khd->qhd", probs_low, value_heads, preferred_element_type=jnp.float32)
    delta_rows = jnp.sum(grad_heads.astype(jnp.float32) * context, axis=-1)
    prob_grad = jnp.einsum(
        "qhd,khd->hqk", grad_heads, value_heads, preferred_element_type=jnp.float32
    )
    score_grad = (probabilities * (prob_grad - delta_rows.T[:, :, None]) * score_scale).astype(
        jnp.bfloat16
    )
    query_grad = jnp.einsum(
        "hqk,khd->qhd", score_grad, key_heads, preferred_element_type=jnp.float32
    )
    key_grad = jnp.einsum(
        "hqk,qhd->khd", score_grad, query_heads, preferred_element_type=jnp.float32
    )
    value_grad = jnp.einsum(
        "hqk,qhd->khd", probs_low, grad_heads, preferred_element_type=jnp.float32
    )
    width = query_rows.shape[1]
    return (
        query_grad.astype(jnp.bfloat16).reshape(query_count, width),
        key_grad.astype(jnp.bfloat16).reshape(state_count, width),
        value_grad.astype(jnp.bfloat16).reshape(state_count, width),
    )


def shards(
    queries, states, state_doc, state_pos, lengths, offsets, key_weight, value_weight, context_grad
):
    seq_count = lax.axis_size("seq")
    device = lax.axis_index("seq")
    row_count = states.shape[0]
    capacity = 3 * row_count // (4 * seq_count) + row_count // 16
    docs_all = state_doc.reshape(seq_count, row_count)
    positions_all = state_pos.reshape(seq_count, row_count)
    onehot = (docs_all[:, :, None] == jnp.arange(seq_count)[None, None, :]).astype(jnp.int32)
    earlier = jnp.cumsum(onehot, axis=1) - onehot
    slots_all = jnp.sum(earlier * onehot, axis=2)
    own_docs = lax.dynamic_index_in_dim(docs_all, device, 0, keepdims=False)
    own_slots = lax.dynamic_index_in_dim(slots_all, device, 0, keepdims=False)
    targets = own_docs * capacity + own_slots
    source_row = jnp.full((seq_count * capacity,), row_count, jnp.int32)
    source_row = source_row.at[targets].set(jnp.arange(row_count, dtype=jnp.int32))
    arrival_index = jnp.arange(seq_count, dtype=jnp.int32)[:, None] * capacity + slots_all
    placed = jnp.where(docs_all == device, positions_all, row_count)
    order_slot = jnp.zeros((row_count,), jnp.int32)
    order_slot = order_slot.at[placed.reshape(-1)].set(arrival_index.reshape(-1), mode="drop")
    padded = jnp.concatenate([states, jnp.zeros((1, states.shape[1]), states.dtype)], axis=0)
    arrived = lax.all_to_all(
        jnp.take(padded, source_row, axis=0), "seq", split_axis=0, concat_axis=0, tiled=True
    )
    doc_states = lax.all_gather(jnp.take(arrived, order_slot, axis=0), "tp", axis=1, tiled=True)
    key_rows = jnp.dot(doc_states, key_weight, preferred_element_type=jnp.float32).astype(
        jnp.bfloat16
    )
    value_rows = jnp.dot(doc_states, value_weight, preferred_element_type=jnp.float32).astype(
        jnp.bfloat16
    )
    length = lax.dynamic_index_in_dim(lengths, device, 0, keepdims=False)
    offset = lax.dynamic_index_in_dim(offsets, device, 0, keepdims=False)
    query_grad, key_grad, value_grad = attend(
        queries, key_rows, value_rows, context_grad, length, offset
    )
    both_grads = jnp.concatenate([key_grad, value_grad], axis=1)
    summed = lax.psum_scatter(
        lax.dot_general(
            doc_states, both_grads, (((0,), (0,)), ((), ())), preferred_element_type=jnp.float32
        ).astype(jnp.bfloat16),
        "seq",
        scatter_dimension=0,
        tiled=True,
    ).astype(jnp.float32)
    head_width = key_weight.shape[1]
    return (
        query_grad,
        summed[:, :head_width].astype(jnp.bfloat16),
        summed[:, head_width:].astype(jnp.bfloat16),
    )


def solution(mesh):
    in_specs = (
        P("seq", "tp"),
        P("seq", "tp"),
        P(),
        P(),
        P(),
        P(),
        P(None, "tp"),
        P(None, "tp"),
        P("seq", "tp"),
    )
    out_specs = (P("seq", "tp"), P("seq", "tp"), P("seq", "tp"))
    return jax.shard_map(shards, mesh=mesh, in_specs=in_specs, out_specs=out_specs, check_vma=False)
```

profile of v0, /device:TPU:1, one launch (start us, length us, event | category | flops | bytes accessed | tf_op | source)
XLA Modules:
  0.0 280.3 jit_solution(13392253341646939702)
XLA Ops:
  7.2 0.8 eq.34
  8.0 0.8 fusion.16
  8.8 18.1 %reduce-window.6 = s32[16,16,4,128]{3,1,2,0:T(8,128)S(1)} reduce-window(s32[16,16,4,128]{3,1,2,0:T(8,128)S(1)} %fusion.16, s32[]{:T(128)} %constant.34.clone.1), window={size=1x1x1x128 pad=0_0x0_0x0_0x127_0}, to_apply=%region_0.0 | reduce-window | flops 16646144 | bytes 1048580 | tf_op jit(solution)/shard_map/reduce-window
  27.0 0.2 slice.22
  27.2 0.4 copy.25
  27.6 0.1 fusion.20
  27.8 0.2 fusion.15
  28.1 2.4 scatter_custom_fusion.1
  30.5 0.1 broadcast_in_dim.63
  30.7 0.0 copy-start.7
  30.7 0.0 copy-start.8
  30.7 3.5 %gather_fusion = bf16[896,512]{1,0:T(8,128)(2,1)S(1)} fusion(bf16[513,512]{1,0:T(8,128)(2,1)S(1)} %concatenate.6, s32[1024]{0:T(1024)S(1)} %pad_clamp_fusion.1), kind=kCustom, calls=%fused_computation | custom fusion | bytes 1838592 | tf_op jit(solution)/shard_map/jit(_take)/gather | solution.py:78
  34.2 1.1 broadcast_select_fusion
  35.4 8.5 %all-to-all-start = ((bf16[16,56,512]{2,1,0:T(8,128)(2,1)}), bf16[16,56,512]{2,1,0:T(8,128)(2,1)S(1)}, u32[]{:S(2)}, u32[]{:S(2)}) async-start(bf16[16,56,512]{2,1,0:T(8,128)(2,1)} %broadcast_select_fusion), calls=%async_computation | async-start | bytes 1835008 | tf_op jit(solution)/shard_map/all_to_all | solution.py:77
  43.9 0.0 copy-start.5
  43.9 0.0 all-gather.2.cloned.1.call-start
  44.0 0.1 add_bitcast_fusion.1
  44.1 30.4 %scatter_custom_fusion = s32[512]{0:T(512)S(1)} fusion(s32[8192]{0:T(1024)S(1)} %compare_select_fusion, s32[8192]{0:T(1024)S(1)} %bitcast.106, s32[]{:T(128)} %constant.34.clone.1), kind=kCustom, calls=%fused_computation.56 | custom fusion | bytes 2052 | tf_op jit(solution)/shard_map/scatter | solution.py:75
  74.6 2.0 gather_fusion.1
  76.6 0.9 broadcast_select_fusion.1
  77.5 0.0 all-gather.2.cloned.1.call-update
  77.5 0.2 reduce-scatter.2.cloned.1.call-start
  77.8 0.6 dynamic_slice.16
  78.4 0.6 dynamic_slice.17
  79.0 0.2 copy.47
  79.2 0.2 copy.30
  79.4 0.7 iota_compare_fusion.3
  80.0 0.7 iota_add_fusion
  80.7 0.1 fusion.17
  80.8 31.3 %all-gather.2.cloned.1.call-done = bf16[512,4096]{1,0:T(8,128)(2,1)} async-done(((bf16[512,512]{1,0:T(8,128)(2,1)}), bf16[512,4096]{1,0:T(8,128)(2,1)}) %all-gather.2.cloned.1.call-update) | async-done | bytes 4194320 | tf_op jit(solution)/shard_map/all_gather | solution.py:80
  112.2 9.1 %convolution_convert_fusion.1 = bf16[512,1024]{1,0:T(8,128)(2,1)S(1)} fusion(bf16[512,4096]{1,0:T(8,128)(2,1)} %all-gather.2.cloned.1.call-done, bf16[4096,1024]{1,0:T(8,128)(2,1)} %param.16), kind=kOutput, calls=%fused_computation.20 | convolution fusion | flops 4295491584 | bytes 13631488 | tf_op jit(solution)/shard_map/dot_general | solution.py:84
  121.3 0.5 copy.48
  121.9 10.5 %convolution_convert_fusion.2 = bf16[512,1024]{1,0:T(8,128)(2,1)} fusion(bf16[512,4096]{1,0:T(8,128)(2,1)} %all-gather.2.cloned.1.call-done, bf16[4096,1024]{1,0:T(8,128)(2,1)} %param.15), kind=kOutput, calls=%fused_computation.21 | convolution fusion | flops 4295491584 | bytes 13631488 | tf_op jit(solution)/shard_map/dot_general | solution.py:81
  132.4 1.5 copy.46
  133.9 3.4 %fusion.30 = (f32[8,256]{1,0:T(8,128)S(1)}, f32[8,256,512]{1,2,0:T(8,128)}) fusion(pred[256,512]{0,1:T(8,128)(4,1)S(1)} %fusion.17, bf16[512,8,128]{0,2,1:T(8,128)(2,1)S(1)} %bitcast.95, bf16[256,8,128]{0,2,1:T(8,128)(2,1)S(1)} %bitcast.100), kind=kOutput, calls=%fused_computation.63 | convolution fusion | flops 272630272 | bytes 5906432 | tf_op jit(solution)/shard_map/sub | solution.py:27
  137.3 2.5 fusion.10
  139.9 0.8 convolution_convert_fusion.3
  140.7 0.5 fusion.12
  141.2 0.8 copy-done.3
  142.1 2.2 fusion.2
  144.3 0.8 convolution_convert_fusion.4
  145.1 15.8 %convolution_convert_fusion = bf16[4096,2048]{1,0:T(8,128)(2,1)} fusion(bf16[512,4096]{1,0:T(8,128)(2,1)} %all-gather.2.cloned.1.call-done, bf16[512,1024]{0,1:T(8,128)(2,1)S(1)} %bitcast.103, bf16[512,1024]{0,1:T(8,128)(2,1)S(1)} %bitcast.104), kind=kOutput, calls=%fused_computation.5 | convolution fusion | flops 8602517504 | bytes 23068672 | tf_op jit(solution)/shard_map/dot_general | solution.py:94
  160.9 0.0 reduce-scatter.2.cloned.1.call-update
  161.0 1.2 copy-done.1
  162.2 1.3 convolution_convert_fusion.5
  163.4 2.0 copy.40
  165.5 105.7 %reduce-scatter.2.cloned.1.call-done = bf16[256,2048]{1,0:T(8,128)(2,1)} async-done(((bf16[4096,2048]{1,0:T(8,128)(2,1)}), bf16[256,2048]{1,0:T(8,128)(2,1)}) %reduce-scatter.2.cloned.1.call-update) | async-done | bytes 1048592 | tf_op jit(solution)/shard_map/reduce_scatter | solution.py:93
  271.2 2.2 fusion.29
  (32 shorter events, 0.2 us)
Async XLA Ops:
  7.2 23.5 %copy-start.6 = (bf16[512,512]{1,0:T(8,128)(2,1)S(1)}, bf16[512,512]{1,0:T(8,128)(2,1)}, u32[]{:S(2)}) copy-start(bf16[512,512]{1,0:T(8,128)(2,1)} %param.10) | copy-start | bytes 1572868
  30.7 13.4 %copy-start.7 = (s32[8192]{0:T(1024)S(1)}, s32[8192]{0:T(1024)}, u32[]{:S(2)}) copy-start(s32[8192]{0:T(1024)} %param.11) | copy-start | bytes 98308
  30.7 13.4 %copy-start.8 = (s32[8192]{0:T(1024)S(1)}, s32[8192]{0:T(1024)}, u32[]{:S(2)}) copy-start(s32[8192]{0:T(1024)} %param.12) | copy-start | bytes 98308
  35.4 42.4 %copy-start.9 = (s32[16]{0:T(128)S(1)}, s32[16]{0:T(128)}, u32[]{:S(2)}) copy-start(s32[16]{0:T(128)} %param.14) | copy-start | bytes 196
  35.4 43.0 %copy-start.10 = (s32[16]{0:T(128)S(1)}, s32[16]{0:T(128)}, u32[]{:S(2)}) copy-start(s32[16]{0:T(128)} %param.13) | copy-start | bytes 196
  35.4 43.6 %copy-start.4 = (bf16[256,1024]{1,0:T(8,128)(2,1)S(1)}, bf16[256,1024]{1,0:T(8,128)(2,1)}, u32[]{:S(2)}) copy-start(bf16[256,1024]{1,0:T(8,128)(2,1)} %param.9) | copy-start | bytes 1572868
  35.4 39.2 %all-to-all-start = ((bf16[16,56,512]{2,1,0:T(8,128)(2,1)}), bf16[16,56,512]{2,1,0:T(8,128)(2,1)S(1)}, u32[]{:S(2)}, u32[]{:S(2)}) async-start(bf16[16,56,512]{2,1,0:T(8,128)(2,1)} %broadcast_select_fusion), calls=%async_computation | async-start | bytes 1835008 | tf_op jit(solution)/shard_map/all_to_all | solution.py:77
  43.9 35.2 %copy-start.5 = (bf16[256,1024]{1,0:T(8,128)(2,1)S(1)}, bf16[256,1024]{1,0:T(8,128)(2,1)}, u32[]{:S(2)}) copy-start(bf16[256,1024]{1,0:T(8,128)(2,1)} %param.17) | copy-start | bytes 1572868
  43.9 68.2 %all-gather.2.cloned.1.call-start = ((), (), s32[]{:S(2)}) async-start(), calls=%async_computation.2 | async-start | bytes 4718592 | tf_op jit(solution)/shard_map/all_gather | solution.py:80
  77.5 193.7 %reduce-scatter.2.cloned.1.call-start = ((), (), s32[]{:S(2)}) async-start(), calls=%async_computation.3 | async-start | bytes 17825792 | tf_op jit(solution)/shard_map/reduce_scatter | solution.py:93
  121.9 18.8 %copy-start.2 = (bf16[512,1024]{0,1:T(8,128)(2,1)}, bf16[512,1024]{0,1:T(8,128)(2,1)S(1)}, u32[]{:S(2)}) copy-start(bf16[512,1024]{0,1:T(8,128)(2,1)S(1)} %copy.48) | copy-start | bytes 3145732
  133.9 3.5 %copy-start = (bf16[512,1024]{0,1:T(8,128)(2,1)}, bf16[512,1024]{0,1:T(8,128)(2,1)S(1)}, u32[]{:S(2)}) copy-start(bf16[512,1024]{0,1:T(8,128)(2,1)S(1)} %copy.46) | copy-start | bytes 3145732
  139.9 2.2 copy-start.3
  160.9 1.2 copy-start.1
Sparse Core Ops, SparseCore 0:
  77.7 34.4 all-gather.1
  161.1 110.0 reduce-scatter.1
where the time goes:
time: 281 us; the launch traced here: 280 us
  waiting for transfers between devices  137 us (49%)
  local copies, waits for them, and re-layouts  50 us (18%)
  matrix products  44.5 us (16%)
  other arithmetic  25.5 us (9%)
  between operations  14.4 us (5%)
  starting transfers between devices  8.81 us (3%)
    reduce_scatter x1, waiting for transfers between devices, shards(): lax.psum_scatter(lax.dot_general(doc_states, both_grads, (((0,), (0,)), (...  106 us
    all_gather x1, waiting for transfers between devices, shards(): lax.all_gather(jnp.take(arrived, order_slot, axis=0), 'tp', axis=1, tiled...  31.3 us
    scatter x1, local copies, waits for them, and re-layouts, shards(): order_slot.at[placed.reshape(-1)]  30.4 us
    another operation x2, other arithmetic  18.3 us
    dot_general x1, matrix products, shards(): lax.dot_general(doc_states, both_grads, (((0,), (0,)), ((), ())), preferr...  15.8 us
    dot_general x1, matrix products, shards(): jnp.dot(doc_states, key_weight, preferred_element_type=jnp.float32)  10.5 us
    dot_general x1, matrix products, shards(): jnp.dot(doc_states, value_weight, preferred_element_type=jnp.float32)  9.14 us
    all_to_all x1, starting transfers between devices, shards(): lax.all_to_all(jnp.take(padded, source_row, axis=0), 'seq', split_axis=0,...  8.55 us
  transfers between devices with their start and end apart: 3, of which 2 were waited for; matrix products, arithmetic and copies ran while one was open for 13% of the time, Pallas kernels for 0%

commit v1 on v0

--- a/solution.py
+++ b/solution.py
@@ -77,7 +77,13 @@
     arrived = lax.all_to_all(
         jnp.take(padded, source_row, axis=0), "seq", split_axis=0, concat_axis=0, tiled=True
     )
-    doc_states = lax.all_gather(jnp.take(arrived, order_slot, axis=0), "tp", axis=1, tiled=True)
+    local_x = jnp.take(arrived, order_slot, axis=0)
+    heap = []
+    for _ in range(lax.axis_size("tp")):
+        heap.append(local_x)
+    top = jnp.stack(heap, axis=0)
+    piece_now = lax.all_to_all(top, concat_axis=0, axis_name="tp", split_axis=0)
+    doc_states = jnp.concatenate(piece_now, 1)
     key_rows = jnp.dot(doc_states, key_weight, preferred_element_type=jnp.float32).astype(
         jnp.bfloat16
     )

time: 281 us -> 303 us (1.078)
  waiting for transfers between devices: 137 us -> 152 us
  starting transfers between devices: 8.81 us -> 14 us
    all_to_all x0 -> x1, waiting for transfers between devices: none -> 45.7 us  [shards(): piece_now = lax.all_to_all(top, concat_axis=0, axis_name='tp', split_axis=0)]
    all_gather x1 -> x0, waiting for transfers between devices: 31.3 us -> none  [shards(): lax.all_gather(jnp.take(arrived, order_slot, axis=0), 'tp', axis=1, tiled...]
    all_to_all x0 -> x1, starting transfers between devices: none -> 5.56 us  [shards(): piece_now = lax.all_to_all(top, concat_axis=0, axis_name='tp', split_axis=0)]
  transfers between devices with their start and end apart: 3 -> 3, of which waited for: 2 -> 2; matrix products, arithmetic and copies ran while one was open for 13% -> 12% of each run, Pallas kernels for 0% -> 0%
where the time goes in v1:
time: 303 us; the launch traced here: 302 us
  waiting for transfers between devices  152 us (50%)
  local copies, waits for them, and re-layouts  52.5 us (17%)
  matrix products  44.5 us (15%)
  other arithmetic  24.7 us (8%)
  between operations  14.4 us (5%)
  starting transfers between devices  14 us (5%)
    reduce_scatter x1, waiting for transfers between devices, shards(): lax.psum_scatter(lax.dot_general(doc_states, both_grads, (((0,), (0,)), (...  106 us
    all_to_all x1, waiting for transfers between devices, shards(): piece_now = lax.all_to_all(top, concat_axis=0, axis_name='tp', split_axis=0)  45.7 us
    scatter x1, local copies, waits for them, and re-layouts, shards(): order_slot.at[placed.reshape(-1)]  30.4 us
    another operation x2, other arithmetic  18.3 us
    dot_general x1, matrix products, shards(): lax.dot_general(doc_states, both_grads, (((0,), (0,)), ((), ())), preferr...  15.7 us
    dot_general x1, matrix products, shards(): jnp.dot(doc_states, key_weight, preferred_element_type=jnp.float32)  10.5 us
    dot_general x1, matrix products, shards(): jnp.dot(doc_states, value_weight, preferred_element_type=jnp.float32)  9.16 us
    all_to_all x1, starting transfers between devices, shards(): lax.all_to_all(jnp.take(padded, source_row, axis=0), 'seq', split_axis=0,...  8.42 us
  transfers between devices with their start and end apart: 3, of which 2 were waited for; matrix products, arithmetic and copies ran while one was open for 12% of the time, Pallas kernels for 0%

profile of v1, /device:TPU:1, one launch (start us, length us, event | category | flops | bytes accessed | tf_op | source)
XLA Modules:
  0.0 301.9 jit_solution(1820634505876601169)
XLA Ops:
  7.2 0.8 eq.34
  8.0 0.8 fusion.16
  8.8 18.1 %reduce-window.6 = s32[16,16,4,128]{3,1,2,0:T(8,128)S(1)} reduce-window(s32[16,16,4,128]{3,1,2,0:T(8,128)S(1)} %fusion.16, s32[]{:T(128)} %constant.34.clone.1), window={size=1x1x1x128 pad=0_0x0_0x0_0x127_0}, to_apply=%region_0.0 | reduce-window | flops 16646144 | bytes 1048580 | tf_op jit(solution)/shard_map/reduce-window
  27.0 0.2 slice.22
  27.2 0.4 copy.25
  27.6 0.1 fusion.20
  27.8 0.2 fusion.15
  28.1 2.4 scatter_custom_fusion.1
  30.6 0.1 broadcast_in_dim.63
  30.7 0.0 copy-start.7
  30.7 0.0 copy-start.8
  30.7 3.5 %gather_fusion = bf16[896,512]{1,0:T(8,128)(2,1)S(1)} fusion(bf16[513,512]{1,0:T(8,128)(2,1)S(1)} %concatenate.6, s32[1024]{0:T(1024)S(1)} %pad_clamp_fusion.1), kind=kCustom, calls=%fused_computation | custom fusion | bytes 1838592 | tf_op jit(solution)/shard_map/jit(_take)/gather | solution.py:78
  34.2 1.1 broadcast_select_fusion
  35.4 8.4 %all-to-all-start = ((bf16[16,56,512]{2,1,0:T(8,128)(2,1)}), bf16[16,56,512]{2,1,0:T(8,128)(2,1)S(1)}, u32[]{:S(2)}, u32[]{:S(2)}) async-start(bf16[16,56,512]{2,1,0:T(8,128)(2,1)} %broadcast_select_fusion), calls=%async_computation | async-start | bytes 1835008 | tf_op jit(solution)/shard_map/all_to_all | solution.py:77
  43.8 0.1 add_bitcast_fusion.1
  43.9 30.4 %scatter_custom_fusion = s32[512]{0:T(512)S(1)} fusion(s32[8192]{0:T(1024)S(1)} %compare_select_fusion, s32[8192]{0:T(1024)S(1)} %bitcast.109, s32[]{:T(128)} %constant.34.clone.1), kind=kCustom, calls=%fused_computation.56 | custom fusion | bytes 2052 | tf_op jit(solution)/shard_map/scatter | solution.py:75
  74.4 2.0 gather_fusion.1
  76.4 0.1 broadcast_select_fusion.1
  76.5 0.2 copy.28
  76.8 2.3 stack.2
  79.1 5.6 %all-to-all-start.1 = ((bf16[8,512,512]{1,2,0:T(8,128)(2,1)}), bf16[8,512,512]{1,2,0:T(8,128)(2,1)}, u32[]{:S(2)}, u32[]{:S(2)}) async-start(bf16[8,512,512]{1,2,0:T(8,128)(2,1)} %stack.2), calls=%async_computation.1 | async-start | bytes 8388608 | tf_op jit(solution)/shard_map/all_to_all | solution.py:85
  84.6 0.0 reduce-scatter.2.cloned.1.call-start
  84.6 0.6 dynamic_slice.16
  85.2 0.6 dynamic_slice.17
  85.8 0.2 copy.48
  86.0 0.2 copy.31
  86.2 0.7 iota_compare_fusion.3
  86.9 0.7 iota_add_fusion
  87.5 0.1 fusion.17
  87.7 45.7 %all-to-all-done.1 = bf16[8,512,512]{1,2,0:T(8,128)(2,1)} async-done(((bf16[8,512,512]{1,2,0:T(8,128)(2,1)}), bf16[8,512,512]{1,2,0:T(8,128)(2,1)}, u32[]{:S(2)}, u32[]{:S(2)}) %all-to-all-start.1) | async-done | bytes 4194336 | tf_op jit(solution)/shard_map/all_to_all | solution.py:85
  133.4 9.2 %convolution_convert_fusion.1 = bf16[512,1024]{1,0:T(8,128)(2,1)S(1)} fusion(bf16[512,4096]{0,1:T(8,128)(2,1)} %bitcast.8, bf16[4096,1024]{1,0:T(8,128)(2,1)} %param.16), kind=kOutput, calls=%fused_computation.20 | convolution fusion | flops 4295491584 | bytes 13631488 | tf_op jit(solution)/shard_map/dot_general | solution.py:90
  142.6 0.5 copy.49
  143.1 10.5 %convolution_convert_fusion.2 = bf16[512,1024]{1,0:T(8,128)(2,1)} fusion(bf16[512,4096]{0,1:T(8,128)(2,1)} %bitcast.8, bf16[4096,1024]{1,0:T(8,128)(2,1)} %param.15), kind=kOutput, calls=%fused_computation.21 | convolution fusion | flops 4295491584 | bytes 13631488 | tf_op jit(solution)/shard_map/dot_general | solution.py:87
  153.6 1.5 copy.47
  155.2 3.4 %fusion.30 = (f32[8,256]{1,0:T(8,128)S(1)}, f32[8,256,512]{1,2,0:T(8,128)}) fusion(pred[256,512]{0,1:T(8,128)(4,1)S(1)} %fusion.17, bf16[512,8,128]{0,2,1:T(8,128)(2,1)S(1)} %bitcast.98, bf16[256,8,128]{0,2,1:T(8,128)(2,1)S(1)} %bitcast.103), kind=kOutput, calls=%fused_computation.63 | convolution fusion | flops 272630272 | bytes 5906432 | tf_op jit(solution)/shard_map/sub | solution.py:27
  158.6 2.5 fusion.10
  161.1 0.8 convolution_convert_fusion.3
  162.0 0.5 fusion.12
  162.5 0.8 copy-done.3
  163.3 2.2 fusion.2
  165.6 0.8 convolution_convert_fusion.4
  166.4 15.7 %convolution_convert_fusion = bf16[4096,2048]{1,0:T(8,128)(2,1)} fusion(bf16[512,4096]{0,1:T(8,128)(2,1)} %bitcast.8, bf16[512,1024]{0,1:T(8,128)(2,1)S(1)} %bitcast.106, bf16[512,1024]{0,1:T(8,128)(2,1)S(1)} %bitcast.107), kind=kOutput, calls=%fused_computation.5 | convolution fusion | flops 8602517504 | bytes 23068672 | tf_op jit(solution)/shard_map/dot_general | solution.py:100
  182.1 0.0 reduce-scatter.2.cloned.1.call-update
  182.1 1.2 copy-done.1
  183.3 1.3 convolution_convert_fusion.5
  184.6 2.0 copy.41
  186.7 106.2 %reduce-scatter.2.cloned.1.call-done = bf16[256,2048]{1,0:T(8,128)(2,1)} async-done(((bf16[4096,2048]{1,0:T(8,128)(2,1)}), bf16[256,2048]{1,0:T(8,128)(2,1)}) %reduce-scatter.2.cloned.1.call-update) | async-done | bytes 1048592 | tf_op jit(solution)/shard_map/reduce_scatter | solution.py:99
  292.9 2.2 fusion.29
  (33 shorter events, 0.2 us)
Async XLA Ops:
  7.2 23.5 %copy-start.6 = (bf16[512,512]{1,0:T(8,128)(2,1)S(1)}, bf16[512,512]{1,0:T(8,128)(2,1)}, u32[]{:S(2)}) copy-start(bf16[512,512]{1,0:T(8,128)(2,1)} %param.10) | copy-start | bytes 1572868
  30.7 13.2 %copy-start.7 = (s32[8192]{0:T(1024)S(1)}, s32[8192]{0:T(1024)}, u32[]{:S(2)}) copy-start(s32[8192]{0:T(1024)} %param.11) | copy-start | bytes 98308
  30.7 13.2 %copy-start.8 = (s32[8192]{0:T(1024)S(1)}, s32[8192]{0:T(1024)}, u32[]{:S(2)}) copy-start(s32[8192]{0:T(1024)} %param.12) | copy-start | bytes 98308
  35.4 39.0 %all-to-all-start = ((bf16[16,56,512]{2,1,0:T(8,128)(2,1)}), bf16[16,56,512]{2,1,0:T(8,128)(2,1)S(1)}, u32[]{:S(2)}, u32[]{:S(2)}) async-start(bf16[16,56,512]{2,1,0:T(8,128)(2,1)} %broadcast_select_fusion), calls=%async_computation | async-start | bytes 1835008 | tf_op jit(solution)/shard_map/all_to_all | solution.py:77
  79.0 5.6 %copy-start.9 = (s32[16]{0:T(128)S(1)}, s32[16]{0:T(128)}, u32[]{:S(2)}) copy-start(s32[16]{0:T(128)} %param.14) | copy-start | bytes 196
  79.0 6.2 %copy-start.10 = (s32[16]{0:T(128)S(1)}, s32[16]{0:T(128)}, u32[]{:S(2)}) copy-start(s32[16]{0:T(128)} %param.13) | copy-start | bytes 196
  79.0 6.8 %copy-start.4 = (bf16[256,1024]{1,0:T(8,128)(2,1)S(1)}, bf16[256,1024]{1,0:T(8,128)(2,1)}, u32[]{:S(2)}) copy-start(bf16[256,1024]{1,0:T(8,128)(2,1)} %param.9) | copy-start | bytes 1572868
  79.0 7.0 %copy-start.5 = (bf16[256,1024]{1,0:T(8,128)(2,1)S(1)}, bf16[256,1024]{1,0:T(8,128)(2,1)}, u32[]{:S(2)}) copy-start(bf16[256,1024]{1,0:T(8,128)(2,1)} %param.17) | copy-start | bytes 1572868
  79.1 54.3 %all-to-all-start.1 = ((bf16[8,512,512]{1,2,0:T(8,128)(2,1)}), bf16[8,512,512]{1,2,0:T(8,128)(2,1)}, u32[]{:S(2)}, u32[]{:S(2)}) async-start(bf16[8,512,512]{1,2,0:T(8,128)(2,1)} %stack.2), calls=%async_computation.1 | async-start | bytes 8388608 | tf_op jit(solution)/shard_map/all_to_all | solution.py:85
  84.6 208.2 %reduce-scatter.2.cloned.1.call-start = ((), (), s32[]{:S(2)}) async-start(), calls=%async_computation.3 | async-start | bytes 17825792 | tf_op jit(solution)/shard_map/reduce_scatter | solution.py:99
  143.1 18.9 %copy-start.2 = (bf16[512,1024]{0,1:T(8,128)(2,1)}, bf16[512,1024]{0,1:T(8,128)(2,1)S(1)}, u32[]{:S(2)}) copy-start(bf16[512,1024]{0,1:T(8,128)(2,1)S(1)} %copy.49) | copy-start | bytes 3145732
  155.1 3.4 %copy-start = (bf16[512,1024]{0,1:T(8,128)(2,1)}, bf16[512,1024]{0,1:T(8,128)(2,1)S(1)}, u32[]{:S(2)}) copy-start(bf16[512,1024]{0,1:T(8,128)(2,1)S(1)} %copy.47) | copy-start | bytes 3145732
  161.1 2.2 copy-start.3
  182.1 1.2 copy-start.1
Sparse Core Ops, SparseCore 0:
  182.3 110.5 reduce-scatter.1
